TPU v7x, 512 devices: a whole 4x8x8 slice. The times are simulated.
512 devices in a mesh: grp: 16 (over y, core), ops: 32 (over x, z).
Axes of the slice: x: 4, y: 8, z: 8, core: 2. Of those that a mesh axis runs over, the one named last changes fastest.
Arguments:
- op_embed: bfloat16 [131072, 256], P(('grp', 'ops')), may hold values from -6 to 6
- machine_embed: bfloat16 [8192, 256], P('grp'), may hold values from -6 to 6
- cotangent: bfloat16 [131072, 256], P(('grp', 'ops')), may hold values from -6 to 6
- w_query: bfloat16 [256, 256], replicated, may hold values from -0.375 to 0.375
- w_key: bfloat16 [256, 256], replicated, may hold values from -0.375 to 0.375
- w_value: bfloat16 [256, 256], replicated, may hold values from -0.375 to 0.375
- slot_local: int32 [512, 16], P(('grp', 'ops')), may hold values from 0 to 3
- counts: int32 [131072, 16], P(('grp', 'ops')), may hold values from 0 to 128, as said below
Outputs:
- op_grad: bfloat16 [131072, 256], P(('grp', 'ops'))
- machine_grad: float32 [8192, 256], P(('grp', 'ops'))
- grad_wq: float32 [256, 256], replicated
- grad_wk: float32 [256, 256], replicated
- grad_wv: float32 [256, 256], replicated
Inputs may be any that keep to these rules, and one draw needn't show every extreme that they name: The eligible machines of slot e's block for operation o are its first counts[o, e] machines; 0 means the operation has no eligible machine in that block.
All inputs are finite; a program needn't handle non-finite values.
Results may differ from a plain program's by a relative error of at most 0.0056.
Values may be sent and summed in bfloat16 or wider, within the bound.
No kernel may reach another device: no remote copies, remote signals or barrier semaphores. Data moves between devices by JAX's collectives and lax.ppermute only.
A program may use at most 64 MiB of HBM per device.

v0:
```python
import jax
import jax.numpy as jnp
from jax import lax
from jax.sharding import PartitionSpec as P

HEADS = 8
BLK = 128
mean_scale = 0.08838834764831845


def slot_grads(queries, cotangent4, key_rows, value_rows, lengths):
    head_size = queries.shape[2]
    inv_root = head_size ** (-0.5)
    scores = (
        jnp.einsum("ohc,mhc->ohm", queries, key_rows, preferred_element_type=jnp.float32) * inv_root
    )
    sigmoid_score = jax.nn.sigmoid(scores)
    columns = lax.broadcasted_iota(jnp.int32, scores.shape, 2)
    eligible = columns < lengths[:, None, None]
    gates = jnp.where(eligible, sigmoid_score, 0.0).astype(jnp.bfloat16)
    value_dot = jnp.einsum(
        "ohc,mhc->ohm", cotangent4, value_rows, preferred_element_type=jnp.float32
    )
    dscore = jnp.where(
        eligible, mean_scale * value_dot * sigmoid_score * (1.0 - sigmoid_score) * inv_root, 0.0
    ).astype(jnp.bfloat16)
    query_part = jnp.einsum("ohm,mhc->ohc", dscore, key_rows, preferred_element_type=jnp.float32)
    key_grad = jnp.einsum(
        "ohm,ohc->mhc", dscore, queries, preferred_element_type=jnp.float32
    ).astype(jnp.bfloat16)
    value_grad = (
        mean_scale
        * jnp.einsum("ohm,ohc->mhc", gates, cotangent4, preferred_element_type=jnp.float32)
    ).astype(jnp.bfloat16)
    return (query_part, key_grad, value_grad)


def per_device(op_embed, machine_embed, cotangent, w_query, w_key, w_value, slot_local, counts):
    groups = lax.axis_size("grp")
    ops_count = op_embed.shape[0]
    model_width = op_embed.shape[1]
    head_size = model_width // HEADS
    machine_rows = machine_embed.shape[0]
    blocks_here = machine_rows // BLK
    highest = lax.Precision.HIGHEST
    both_weights = jnp.concatenate([w_key, w_value], axis=1)
    queries = jnp.dot(op_embed, w_query, preferred_element_type=jnp.float32).astype(jnp.bfloat16)
    wanted = lax.all_to_all(
        slot_local.reshape(groups, 1), "grp", split_axis=0, concat_axis=0, tiled=True
    )
    wanted_ids = wanted[:, 0]
    picker = wanted_ids[:, None] == jnp.arange(blocks_here, dtype=jnp.int32)[None, :]
    local_pairs = jnp.dot(machine_embed, both_weights, preferred_element_type=jnp.float32).astype(
        jnp.bfloat16
    )
    outgoing = local_pairs.reshape(blocks_here, BLK, 2 * model_width)[wanted_ids]
    fetched = lax.all_to_all(outgoing, "grp", split_axis=0, concat_axis=0, tiled=True)
    key_slots = fetched[:, :, :model_width].reshape(groups, BLK, HEADS, head_size)
    value_slots = fetched[:, :, model_width:].reshape(groups, BLK, HEADS, head_size)
    query_heads = queries.reshape(ops_count, HEADS, head_size)
    cot_heads = cotangent.reshape(ops_count, HEADS, head_size)

    def per_slot(summed_q, pieces):
        key_rows, value_rows, lengths = pieces
        query_part, key_grad, value_grad = slot_grads(
            query_heads, cot_heads, key_rows, value_rows, lengths
        )
        return (
            summed_q + query_part,
            (key_grad.reshape(BLK, model_width), value_grad.reshape(BLK, model_width)),
        )

    start_q = jnp.zeros((ops_count, HEADS, head_size), jnp.float32)
    summed_q, (key_grads, value_grads) = lax.scan(
        per_slot, start_q, (key_slots, value_slots, counts.T)
    )
    grad_query = summed_q.astype(jnp.bfloat16).reshape(ops_count, model_width)
    op_grad = (
        cotangent.astype(jnp.float32)
        + jnp.dot(grad_query, w_query.T, preferred_element_type=jnp.float32)
    ).astype(jnp.bfloat16)
    wq_term = jnp.einsum("od,oe->de", op_embed, grad_query, preferred_element_type=jnp.float32)
    returned = lax.all_to_all(
        jnp.concatenate([key_grads, value_grads], axis=2),
        "grp",
        split_axis=0,
        concat_axis=0,
        tiled=True,
    )
    summed = jnp.einsum(
        "gb,gr->br",
        picker.astype(jnp.bfloat16),
        returned.reshape(groups, BLK * 2 * model_width),
        preferred_element_type=jnp.float32,
    )
    summed = summed.reshape(machine_rows, 2 * model_width)
    key_total = summed[:, :model_width]
    value_total = summed[:, model_width:]
    machine_part = jnp.dot(key_total, w_key.astype(jnp.float32).T, precision=highest) + jnp.dot(
        value_total, w_value.astype(jnp.float32).T, precision=highest
    )
    embed_f = machine_embed.astype(jnp.float32)
    wk_term = jnp.dot(embed_f.T, key_total, precision=highest)
    wv_term = jnp.dot(embed_f.T, value_total, precision=highest)
    summed_total = lax.psum(machine_part, "ops")
    share_rows = machine_rows // lax.axis_size("ops")
    first_row = lax.axis_index("ops") * share_rows
    machine_grad = lax.dynamic_slice_in_dim(summed_total, first_row, share_rows, 0)
    weight_sums = lax.psum((wq_term, wk_term, wv_term), ("grp", "ops"))
    shard_count = float(groups * lax.axis_size("ops"))
    grad_wq = weight_sums[0] / shard_count
    grad_wk = weight_sums[1] / shard_count
    grad_wv = weight_sums[2] / shard_count
    return (op_grad, machine_grad, grad_wq, grad_wk, grad_wv)


def solution(mesh):
    return jax.shard_map(
        per_device,
        mesh=mesh,
        in_specs=(
            P(("grp", "ops"), None),
            P("grp", None),
            P(("grp", "ops"), None),
            P(),
            P(),
            P(),
            P(("grp", "ops"), None),
            P(("grp", "ops"), None),
        ),
        out_specs=(P(("grp", "ops"), None), P(("grp", "ops"), None), P(), P(), P()),
        check_vma=False,
    )
```

profile of v0, /device:TPU:8, one launch (start us, length us, event | category | flops | bytes accessed | tf_op | source)
XLA Modules:
  0.0 657.2 jit_solution(9235457132968034616)
XLA Ops:
  7.2 1.4 copy.46
  8.6 9.1 %all-to-all-start = ((s32[16,1,1]{2,1,0:T(1,128)}), s32[16,1,1]{2,1,0:T(1,128)S(1)}, u32[]{:S(2)}, u32[]{:S(2)}) async-start(s32[16,1,1]{2,1,0:T(1,128)} %copy.46), calls=%async_computation | async-start | bytes 16384 | tf_op jit(solution)/shard_map/all_to_all | solution.py:48
  18.9 4.9 all-to-all-done
  24.2 2.0 gather_fusion
  26.2 5.1 all-to-all-start.1
  31.7 46.8 %all-to-all-done.1 = bf16[16,128,512]{2,1,0:T(8,128)(2,1)S(1)} async-done(((bf16[16,128,512]{2,1,0:T(8,128)(2,1)}), bf16[16,128,512]{2,1,0:T(8,128)(2,1)S(1)}, u32[]{:S(2)}, u32[]{:S(2)}) %all-to-all-start.1) | async-done | bytes 2097184 | tf_op jit(solution)/shard_map/all_to_all | solution.py:57
  78.6 1.6 fusion.38
  80.2 1.7 copy.47
  81.9 1.3 copy.48
  83.2 63.6 %while.15 = (s32[]{:T(128)}, f32[256,8,32]{0,2,1:T(8,128)S(1)}, bf16[16,128,256]{1,2,0:T(8,128)(2,1)}, bf16[16,128,256]{1,2,0:T(8,128)(2,1)}, bf16[16,128,8,32]{...) while((s32[]{:T(128)}, f32[256,8,32]{0,2,1:T(8,128)S(1)}, ...), condition=%wide.region_1.2_spmd.clone, body=%wide.region_0.1_spmd.clone.sunk | while | flops 87785472 | bytes 6361235 | solution.py:74
  84.4 1.3 fusion.80
  88.4 1.3 fusion.80
  92.4 1.3 fusion.80
  96.3 1.3 fusion.80
  100.3 1.3 fusion.80
  104.3 1.3 fusion.80
  108.2 1.3 fusion.80
  112.2 1.3 fusion.80
  116.2 1.3 fusion.80
  120.2 1.3 fusion.80
  124.1 1.3 fusion.80
  128.1 1.3 fusion.80
  132.1 1.3 fusion.80
  140.1 1.3 fusion.80
  144.0 1.3 fusion.80
  146.8 3.1 pad_maximum_fusion
  149.9 6.9 %all-to-all-start.2 = ((bf16[16,128,512]{1,2,0:T(8,128)(2,1)}), bf16[16,128,512]{1,2,0:T(8,128)(2,1)}, u32[]{:S(2)}, u32[]{:S(2)}) async-start(bf16[16,128,512]{1,2,0:T(8,128)(2,1)} %pad_maximum_fusion), calls=%async_computation.2 | async-start | bytes 4194304 | tf_op jit(solution)/shard_map/all_to_all | solution.py:83
  157.7 46.3 %all-to-all-done.2 = bf16[16,128,512]{1,2,0:T(8,128)(2,1)} async-done(((bf16[16,128,512]{1,2,0:T(8,128)(2,1)}), bf16[16,128,512]{1,2,0:T(8,128)(2,1)}, u32[]{:S(2)}, u32[]{:S(2)}) %all-to-all-start.2) | async-done | bytes 2097184 | tf_op jit(solution)/shard_map/all_to_all | solution.py:83
  204.0 3.4 copy.57
  214.0 274.6 %all-reduce.6.cloned.1.call-done = (f32[256,256]{0,1:T(8,128)}, f32[256,256]{0,1:T(8,128)}, f32[256,256]{0,1:T(8,128)}) async-done(((f32[256,256]{0,1:T(8,128)}, f32[256,256]{0,1:T(8,128)}, f32[256,256]{0,1:T(8,128)}), (f32[256,256]{0,1:T(8,128)}, f32[256,256]{0,1:T(8,128)}, f32[256,256]{0,1:T(8,128)})) %all-reduce.6.cloned.1.call-update) | async-done | bytes 786448 | tf_op jit(solution)/shard_map/psum | solution.py:109
  493.2 155.8 %all-reduce.4.cloned.1.call-done = f32[512,256]{1,0:T(8,128)} async-done(((f32[512,256]{1,0:T(8,128)}), f32[512,256]{1,0:T(8,128)}) %all-reduce.4.cloned.1.call-update) | async-done | bytes 524304 | tf_op jit(solution)/shard_map/psum | solution.py:105
  649.0 1.3 constant_dynamic-slice_fusion.1
  (144 shorter events, 57.5 us)
Async XLA Ops:
  7.2 10.5 %copy-start = (bf16[512,256]{1,0:T(8,128)(2,1)S(1)}, bf16[512,256]{1,0:T(8,128)(2,1)}, u32[]{:S(2)}) copy-start(bf16[512,256]{1,0:T(8,128)(2,1)} %param.11) | copy-start | bytes 786436
  8.6 15.3 %all-to-all-start = ((s32[16,1,1]{2,1,0:T(1,128)}), s32[16,1,1]{2,1,0:T(1,128)S(1)}, u32[]{:S(2)}, u32[]{:S(2)}) async-start(s32[16,1,1]{2,1,0:T(1,128)} %copy.46), calls=%async_computation | async-start | bytes 16384 | tf_op jit(solution)/shard_map/all_to_all | solution.py:48
  26.2 5.1 copy-start.6
  26.2 5.3 copy-start.2
  26.2 5.3 copy-start.4
  26.2 52.3 %all-to-all-start.1 = ((bf16[16,128,512]{2,1,0:T(8,128)(2,1)}), bf16[16,128,512]{2,1,0:T(8,128)(2,1)S(1)}, u32[]{:S(2)}, u32[]{:S(2)}) async-start(bf16[16,128,512]{2,1,0:T(8,128)(2,1)} %gather_fusion), calls=%async_computation.1 | async-start | bytes 4194304 | tf_op jit(solution)/shard_map/all_to_all | solution.py:57
  80.2 1.7 copy-start.1
  149.9 6.9 %copy-start.3 = (bf16[256,256]{1,0:T(8,128)(2,1)S(1)}, bf16[256,256]{1,0:T(8,128)(2,1)}, u32[]{:S(2)}) copy-start(bf16[256,256]{1,0:T(8,128)(2,1)} %param.10) | copy-start | bytes 393220
  149.9 54.2 %all-to-all-start.2 = ((bf16[16,128,512]{1,2,0:T(8,128)(2,1)}), bf16[16,128,512]{1,2,0:T(8,128)(2,1)}, u32[]{:S(2)}, u32[]{:S(2)}) async-start(bf16[16,128,512]{1,2,0:T(8,128)(2,1)} %pad_maximum_fusion), calls=%async_computation.2 | async-start | bytes 4194304 | tf_op jit(solution)/shard_map/all_to_all | solution.py:83
  156.8 331.9 %all-reduce.6.cloned.1.call-start = ((), (), s32[]{:S(2)}) async-start(), calls=%async_computation.4 | async-start | bytes 1572864 | tf_op jit(solution)/shard_map/psum | solution.py:109
  208.0 3.4 copy-start.8
  208.7 3.1 copy-start.9
  211.3 1.8 copy-start.5
  211.3 1.8 copy-start.7
  211.4 437.6 %all-reduce.4.cloned.1.call-start = ((), (), s32[]{:S(2)}) async-start(), calls=%async_computation.3 | async-start | bytes 1048576 | tf_op jit(solution)/shard_map/psum | solution.py:105
Sparse Core Ops, SparseCore 0:
  211.5 277.0 all-reduce.5
  492.0 156.9 all-reduce.3
where the time goes:
time: 659 us; the launch traced here: 657 us
  waiting for transfers between devices  529 us (80%)
  matrix products  48.8 us (7%)
  local copies, waits for them, and re-layouts  38.4 us (6%)
  starting transfers between devices  21.1 us (3%)
  between operations  14.3 us (2%)
    psum x1, waiting for transfers between devices, per_device(): weight_sums = lax.psum((wq_term, wk_term, wv_term), ('grp', 'ops'))  275 us
    psum x1, waiting for transfers between devices, per_device(): summed_total = lax.psum(machine_part, 'ops')  156 us
    all_to_all x1, waiting for transfers between devices, per_device(): lax.all_to_all(outgoing, 'grp', split_axis=0, concat_axis=0, tiled=True)  46.8 us
    all_to_all x1, waiting for transfers between devices, per_device(): lax.all_to_all(jnp.concatenate([key_grads, value_grads], axis=2), 'grp',...  46.3 us
    dot_general x16, matrix products, slot_grads(): jnp.einsum('ohc,mhc->ohm', cotangent4, value_rows, preferred_element_type...  20.9 us
  transfers between devices with their start and end apart: 5, of which 5 were waited for; matrix products, arithmetic and copies ran while one was open for 1% of the time, Pallas kernels for 0%

commit v1 on v0

--- a/solution.py
+++ b/solution.py
@@ -2,6 +2,7 @@
 import jax.numpy as jnp
 from jax import lax
 from jax.sharding import PartitionSpec as P
+from jax.lax import psum
 
 HEADS = 8
 BLK = 128
@@ -106,7 +107,7 @@
     share_rows = machine_rows // lax.axis_size("ops")
     first_row = lax.axis_index("ops") * share_rows
     machine_grad = lax.dynamic_slice_in_dim(summed_total, first_row, share_rows, 0)
-    weight_sums = lax.psum((wq_term, wk_term, wv_term), ("grp", "ops"))
+    weight_sums = psum(psum((wq_term, wk_term, wv_term), "ops"), "grp")
     shard_count = float(groups * lax.axis_size("ops"))
     grad_wq = weight_sums[0] / shard_count
     grad_wk = weight_sums[1] / shard_count

time: 659 us -> 523 us (0.79)
  the two profiles are of different devices: /device:TPU:8 before, /device:TPU:1 now
where the time goes in v1:
time: 523 us; the launch traced here: 521 us
  waiting for transfers between devices  380 us (73%)
  matrix products  62.4 us (12%)
  local copies, waits for them, and re-layouts  37.5 us (7%)
  starting transfers between devices  20 us (4%)
  between operations  14.2 us (3%)
  other arithmetic  5.53 us (1%)
    psum x1, waiting for transfers between devices, per_device(): summed_total = lax.psum(machine_part, 'ops')  159 us
    psum x1, waiting for transfers between devices, per_device(): weight_sums = psum(psum((wq_term, wk_term, wv_term), 'ops'), 'grp')  119 us
    all_to_all x1, waiting for transfers between devices, per_device(): lax.all_to_all(outgoing, 'grp', split_axis=0, concat_axis=0, tiled=True)  48.8 us
    all_to_all x1, waiting for transfers between devices, per_device(): lax.all_to_all(jnp.concatenate([key_grads, value_grads], axis=2), 'grp',...  48.2 us
    dot_general x16, matrix products, slot_grads(): jnp.einsum('ohc,mhc->ohm', queries, key_rows, preferred_element_type=jnp....  21.3 us
    dot_general x16, matrix products, slot_grads(): jnp.einsum('ohm,mhc->ohc', dscore, key_rows, preferred_element_type=jnp.f...  16.9 us
    dynamic_slice x16, local copies, waits for them, and re-layouts, per_device(): lax.scan(per_slot, start_q, (key_slots, value_slots, counts.T))  11.3 us
    dynamic_update_slice x16, local copies, waits for them, and re-layouts, per_device(): lax.scan(per_slot, start_q, (key_slots, value_slots, counts.T))  11 us
  transfers between devices with their start and end apart: 5, of which 5 were waited for; matrix products, arithmetic and copies ran while one was open for 1% of the time, Pallas kernels for 0%

profile of v1, /device:TPU:1, one launch (start us, length us, event | category | flops | bytes accessed | tf_op | source)
XLA Modules:
  0.0 520.6 jit_solution(15627018179011689782)
XLA Ops:
  7.2 1.4 copy.46
  8.6 10.1 %all-to-all-start = ((s32[16,1,1]{2,1,0:T(1,128)}), s32[16,1,1]{2,1,0:T(1,128)S(1)}, u32[]{:S(2)}, u32[]{:S(2)}) async-start(s32[16,1,1]{2,1,0:T(1,128)} %copy.46), calls=%async_computation | async-start | bytes 16384 | tf_op jit(solution)/shard_map/all_to_all | solution.py:49
  19.9 5.7 %all-to-all-done = s32[16,1,1]{2,1,0:T(1,128)S(1)} async-done(((s32[16,1,1]{2,1,0:T(1,128)}), s32[16,1,1]{2,1,0:T(1,128)S(1)}, u32[]{:S(2)}, u32[]{:S(2)}) %all-to-all-start) | async-done | bytes 96 | tf_op jit(solution)/shard_map/all_to_all | solution.py:49
  26.1 2.0 gather_fusion
  28.1 5.0 all-to-all-start.1
  33.4 48.8 %all-to-all-done.1 = bf16[16,128,512]{2,1,0:T(8,128)(2,1)} async-done(((bf16[16,128,512]{2,1,0:T(8,128)(2,1)}), bf16[16,128,512]{2,1,0:T(8,128)(2,1)}, u32[]{:S(2)}, u32[]{:S(2)}) %all-to-all-start.1) | async-done | bytes 2097184 | tf_op jit(solution)/shard_map/all_to_all | solution.py:58
  82.2 1.7 fusion.38
  83.9 1.3 copy.47
  85.9 77.1 %while.15 = (s32[]{:T(128)}, f32[256,8,32]{0,2,1:T(8,128)S(1)}, bf16[16,128,256]{1,2,0:T(8,128)(2,1)}, bf16[16,128,256]{1,2,0:T(8,128)(2,1)}, bf16[16,128,8,32]{...) while((s32[]{:T(128)}, f32[256,8,32]{0,2,1:T(8,128)S(1)}, ...), condition=%wide.region_1.2_spmd.clone, body=%wide.region_0.1_spmd.clone.sunk | while | flops 87785472 | bytes 6361235 | solution.py:75
  85.9 1.3 fusion.79
  90.7 1.3 fusion.79
  95.6 1.3 fusion.79
  100.4 1.3 fusion.79
  105.2 1.3 fusion.79
  110.0 1.3 fusion.79
  114.8 1.3 fusion.79
  119.7 1.3 fusion.79
  124.5 1.3 fusion.79
  129.3 1.3 fusion.79
  134.1 1.3 fusion.79
  138.9 1.3 fusion.79
  143.8 1.3 fusion.79
  148.6 1.3 fusion.79
  153.4 1.3 fusion.79
  158.2 1.3 fusion.79
  163.0 3.1 pad_maximum_fusion
  166.1 4.8 all-to-all-start.2
  171.9 48.2 %all-to-all-done.2 = bf16[16,128,512]{1,2,0:T(8,128)(2,1)} async-done(((bf16[16,128,512]{1,2,0:T(8,128)(2,1)}), bf16[16,128,512]{1,2,0:T(8,128)(2,1)}, u32[]{:S(2)}, u32[]{:S(2)}) %all-to-all-start.2) | async-done | bytes 2097184 | tf_op jit(solution)/shard_map/all_to_all | solution.py:84
  220.1 3.4 copy.57
  229.3 159.0 %all-reduce.5.cloned.1.call-done = (f32[512,256]{1,0:T(8,128)}, f32[256,256]{0,1:T(8,128)}, f32[256,256]{0,1:T(8,128)}, f32[256,256]{0,1:T(8,128)}) async-done(((f32[512,256]{1,0:T(8,128)}, f32[256,256]{0,1:T(8,128)}, f32[256,256]{0,1:T(8,128)}, f32[256,256]{0,1:T(8,128)}), (f32[512,256]{1,0:T(8,128)}, f32[256,256]{0,1:T(8,128)}, f32[256,256]{0,1:T(8,128)}, ...) | async-done | bytes 1310736 | tf_op jit(solution)/shard_map/psum | solution.py:106
  389.3 1.3 constant_dynamic-slice_fusion.1
  390.6 118.6 %all-reduce.7.cloned.1.call-done = (f32[256,256]{0,1:T(8,128)}, f32[256,256]{0,1:T(8,128)}, f32[256,256]{0,1:T(8,128)}) async-done(((f32[256,256]{0,1:T(8,128)}, f32[256,256]{0,1:T(8,128)}, f32[256,256]{0,1:T(8,128)}), (f32[256,256]{0,1:T(8,128)}, f32[256,256]{0,1:T(8,128)}, f32[256,256]{0,1:T(8,128)})) %all-reduce.7.cloned.1.call-update) | async-done | bytes 786448 | tf_op jit(solution)/shard_map/psum | solution.py:110
  (140 shorter events, 70.2 us)
Async XLA Ops:
  7.2 11.5 %copy-start = (bf16[512,256]{1,0:T(8,128)(2,1)S(1)}, bf16[512,256]{1,0:T(8,128)(2,1)}, u32[]{:S(2)}) copy-start(bf16[512,256]{1,0:T(8,128)(2,1)} %param.11) | copy-start | bytes 786436
  8.6 17.1 %all-to-all-start = ((s32[16,1,1]{2,1,0:T(1,128)}), s32[16,1,1]{2,1,0:T(1,128)S(1)}, u32[]{:S(2)}, u32[]{:S(2)}) async-start(s32[16,1,1]{2,1,0:T(1,128)} %copy.46), calls=%async_computation | async-start | bytes 16384 | tf_op jit(solution)/shard_map/all_to_all | solution.py:49
  28.1 5.0 copy-start.4
  28.1 5.1 copy-start.1
  28.1 5.1 copy-start.2
  28.1 54.2 %all-to-all-start.1 = ((bf16[16,128,512]{2,1,0:T(8,128)(2,1)}), bf16[16,128,512]{2,1,0:T(8,128)(2,1)}, u32[]{:S(2)}, u32[]{:S(2)}) async-start(bf16[16,128,512]{2,1,0:T(8,128)(2,1)} %gather_fusion), calls=%async_computation.1 | async-start | bytes 4194304 | tf_op jit(solution)/shard_map/all_to_all | solution.py:58
  166.1 54.0 %all-to-all-start.2 = ((bf16[16,128,512]{1,2,0:T(8,128)(2,1)}), bf16[16,128,512]{1,2,0:T(8,128)(2,1)}, u32[]{:S(2)}, u32[]{:S(2)}) async-start(bf16[16,128,512]{1,2,0:T(8,128)(2,1)} %pad_maximum_fusion), calls=%async_computation.2 | async-start | bytes 4194304 | tf_op jit(solution)/shard_map/all_to_all | solution.py:84
  171.0 217.4 %all-reduce.5.cloned.1.call-start = ((), (), s32[]{:S(2)}) async-start(), calls=%async_computation.3 | async-start | bytes 2621440 | tf_op jit(solution)/shard_map/psum | solution.py:106
  224.1 0.9 copy-start.6
  225.0 3.0 copy-start.7
  228.0 160.4 %copy-start.3 = (bf16[256,256]{1,0:T(8,128)(2,1)S(1)}, bf16[256,256]{1,0:T(8,128)(2,1)}, u32[]{:S(2)}) copy-start(bf16[256,256]{1,0:T(8,128)(2,1)} %param.13) | copy-start | bytes 393220
  228.0 160.4 %copy-start.5 = (bf16[256,256]{1,0:T(8,128)(2,1)S(1)}, bf16[256,256]{1,0:T(8,128)(2,1)}, u32[]{:S(2)}) copy-start(bf16[256,256]{1,0:T(8,128)(2,1)} %param.12) | copy-start | bytes 393220
  229.2 279.9 %all-reduce.7.cloned.1.call-start = ((), (), s32[]{:S(2)}) async-start(), calls=%async_computation.4 | async-start | bytes 1572864 | tf_op jit(solution)/shard_map/psum | solution.py:110
Sparse Core Ops, SparseCore 0:
  229.4 158.9 all-reduce.4
  390.8 118.2 all-reduce.6
